TPU v7x, 32 devices: a whole 2x2x4 slice. The times are simulated.
32 devices in a mesh: grp: 2 (over x), chan: 16 (over z, y, core).
Axes of the slice: x: 2, y: 2, z: 4, core: 2. Of those that a mesh axis runs over, the one named last changes fastest.
Arguments:
- spectra: bfloat16 [128, 4, 2, 4096], P(('grp', 'chan')), parts along dimension 0, may hold values from -60 to 60
- valid: int32 [128, 4], P(('grp', 'chan')), parts along dimension 0, may hold values 0 or 1
- partner: int32 [16], replicated, may hold values from 0 to 15, as said below
- pair_bin: int32 [1024], P(('grp', 'chan')), parts along dimension 0, may hold values from -1 to 127, as said below
- pair_count: int32 [32], P(('grp', 'chan')), parts along dimension 0, may hold values from 24 to 32
Outputs:
- stacked: float32 [256, 1024], P(('grp', 'chan')), parts along dimension 0
There are 2 independent parts, one for each index of `grp`. A program takes and returns all parts, laid end to end along the dimension named above; an argument that names none is the same for every part. Nothing has to cross between parts.
Inputs may be any that keep to these rules, and one draw needn't show every extreme that they name: partner[p] = p XOR r for one r of 1 to 15, the same for every p. `pair_bin`: -1 marks a row without bin, and every row pairing a channel with itself is -1; bin k is owned by block k // 8.
All inputs are finite; a program needn't handle non-finite values. No bound on the sum of `valid` on one device may be relied on, other than what follows from the above.
Results may differ from a plain program's by a relative error of at most 0.0056.
Values may be sent and summed in bfloat16 or wider, within the bound.
A program may use at most 128 MiB of HBM per device.

v0:
```python
import functools
import math

import jax
import jax.numpy as jnp
import ml_dtypes
import numpy as np
from jax import lax
from jax.experimental import pallas as pl
from jax.experimental.pallas import tpu as pltpu
from jax.sharding import PartitionSpec as P

F = 4096
BAND = 128
LAGS = 1024
BINS_DEV = 8
PAIRS_DEV = 32
LANES = 128
GROUP = 4


def from_partner(block, axis, bit):
    count = lax.axis_size(axis)
    route = []
    for low in range(count):
        high = low | 1 << bit
        if high != low and high < count:
            route += [(low, high), (high, low)]
    return lax.ppermute(block, axis, route)


def whiten(spectra, valid):
    values = spectra.astype(jnp.float32)
    power = values[:, :, 0] * values[:, :, 0] + values[:, :, 1] * values[:, :, 1]
    nchan, nwin, nfreq = power.shape
    banded = jnp.mean(power.reshape(nchan, nwin, nfreq // BAND, BAND), axis=-1)
    amplitude = jnp.repeat(jnp.sqrt(banded + 1e-06), BAND, axis=-1)
    weights = valid.astype(jnp.float32)[:, :, None, None]
    return (values * weights / amplitude[:, :, None, :]).astype(jnp.bfloat16)


def lag_table():
    freqs = jnp.arange(F, dtype=jnp.int32)
    shifts = jnp.arange(LAGS, dtype=jnp.int32) - LAGS // 2
    phase = jnp.mod(freqs[:, None] * shifts[None, :], 2 * F)
    angle = phase.astype(jnp.float32) * (2.0 * math.pi / (2 * F))
    scale = 1.0 / math.sqrt(F)
    return jnp.concatenate([jnp.cos(angle) * scale, -jnp.sin(angle) * scale], axis=0).astype(
        jnp.bfloat16
    )


def cross_product(left_part, right_part):
    return jnp.einsum("awf,bwf->abf", left_part, right_part, preferred_element_type=jnp.float32)


def correlate(own_block, other_block, table):
    own_real = own_block[:, :, 0]
    own_imag = own_block[:, :, 1]
    oth_real = other_block[:, :, 0]
    oth_imag = other_block[:, :, 1]
    real_part = cross_product(own_real, oth_real) + cross_product(own_imag, oth_imag)
    imag_part = cross_product(own_imag, oth_real) - cross_product(own_real, oth_imag)
    nchan = own_block.shape[0]
    nwin = own_block.shape[1]
    spec = (jnp.concatenate([real_part, imag_part], axis=-1) * (1.0 / nwin)).reshape(
        nchan * nchan, -1
    )
    spec = spec.astype(jnp.bfloat16)
    return jnp.dot(spec, table, preferred_element_type=jnp.float32)


def select_sum(selector, corr_high, corr_low):
    return jnp.dot(selector, corr_high, preferred_element_type=jnp.float32) + jnp.dot(
        selector, corr_low, preferred_element_type=jnp.float32
    )


def on_device_blocks(spectra, valid, partner, pair_bin, pair_count):
    white = whiten(spectra, valid)
    nblocks = lax.axis_size("chan")
    round_mask = partner[0]
    paired = white
    for bit_index in range(nblocks.bit_length() - 1):
        swapped = from_partner(paired, "chan", bit_index)
        paired = jnp.where(round_mask >> bit_index & 1 == 1, swapped, paired)
    table = lag_table()
    self_corr = correlate(white, white, table)
    cross_corr = correlate(white, paired, table)
    corr = jnp.concatenate([self_corr, cross_corr], axis=0)
    corr_high = corr.astype(jnp.bfloat16)
    corr_low = (corr - corr_high.astype(jnp.float32)).astype(jnp.bfloat16)
    rows = jnp.arange(corr.shape[0], dtype=jnp.int32)
    live_rows = (rows < pair_count[0]) & (pair_bin >= 0)
    kept_bins = jnp.where(live_rows, pair_bin, -1)
    targets = lax.iota(jnp.int32, nblocks * BINS_DEV)
    selector = (kept_bins[None, :] == targets[:, None]).astype(jnp.bfloat16)
    terms = select_sum(selector, corr_high, corr_low).reshape(nblocks, BINS_DEV, -1)
    received = lax.all_to_all(terms, "chan", split_axis=0, concat_axis=0, tiled=True)
    summed = jnp.sum(received, axis=0)
    return summed * (1.0 / math.sqrt(PAIRS_DEV // BINS_DEV))


def base_table(nfreq):
    shifts = np.arange(LAGS) - LAGS // 2
    angle = np.mod(np.arange(nfreq)[:, None] * shifts[None, :], 2 * F) * (2.0 * math.pi / (2 * F))
    cos, sin = np.cos(angle), np.sin(angle)
    return np.concatenate(
        [np.concatenate([cos, sin], axis=1), np.concatenate([-sin, cos], axis=1)], axis=0
    ).astype(ml_dtypes.bfloat16)


def slice_phases(nslices, nfreq, scale):
    shifts = np.arange(LAGS) - LAGS // 2
    first = np.arange(nslices) * nfreq
    angle = np.mod(first[:, None] * shifts[None, :], 2 * F) * (2.0 * math.pi / (2 * F))
    both = np.concatenate([np.cos(angle), -np.sin(angle)], axis=1) * scale
    return both.astype(np.float32)[:, None, :]


def expanders(nchan, nwin):
    row = np.arange(LANES)
    per_chan = 2 * nwin
    step = row // (nchan * per_chan)
    first = row // per_chan % nchan
    window = row // 2 % nwin
    second = (first + step) % nchan
    nvalid = nchan * nwin
    pair = first * nchan + second
    lanes = (
        nvalid + pair,
        nvalid + nchan * nchan + pair,
        first * nwin + window,
        second * nwin + window,
    )
    return np.concatenate(
        [(np.arange(LANES)[:, None] == lane[None, :]) for lane in lanes], axis=1
    ).astype(ml_dtypes.bfloat16)


def swap_pairs(rows):
    size = rows.shape[-2]
    axis = rows.ndim - 2
    even = lax.broadcasted_iota(jnp.int32, rows.shape, axis) % 2 == 0
    return jnp.where(
        even, pltpu.roll(rows, size - 1, axis), pltpu.roll(rows, 1, axis)
    ), even


def kernel(
    dims,
    spectra_ref,
    valid_hbm,
    partner_hbm,
    bin_hbm,
    count_hbm,
    expand_hbm,
    table_hbm,
    phase_hbm,
    out_ref,
    valid_ref,
    partner_ref,
    bin_ref,
    count_ref,
    expand_ref,
    meta_ref,
    raw,
    metas,
    table,
    phases,
    rolled,
    turned,
    kept,
    other_valid,
    selector,
    products,
    self_selector,
    spread_selector,
    self_products,
    totals,
    outgoing,
    incoming,
    local_sems,
    send_a,
    recv_a,
    send_m,
    recv_m,
    send_b,
    recv_b,
):
    n, nchan, nwin, nfreq, nbins_dev = dims
    nrow = nchan * nwin * 2
    nbins = n * nbins_dev
    me = lax.axis_index("chan")
    copy_table = pltpu.make_async_copy(table_hbm, table, local_sems.at[0])
    copy_phase = pltpu.make_async_copy(phase_hbm, phases, local_sems.at[1])

    def mine(target):
        return pl.ds(pl.multiple_of(target * nfreq, nfreq), nfreq)

    own_raw = pltpu.make_async_copy(
        spectra_ref.at[:, :, :, mine(me)], raw.at[me], local_sems.at[2]
    )
    own_meta = pltpu.make_async_copy(meta_ref, metas.at[me], local_sems.at[3])
    small = [
        pltpu.make_async_copy(src, dst, local_sems.at[5 + i])
        for i, (src, dst) in enumerate(
            (
                (valid_hbm, valid_ref),
                (bin_hbm, bin_ref),
                (count_hbm, count_ref),
                (partner_hbm, partner_ref),
                (expand_hbm, expand_ref),
            )
        )
    ]
    for copy in small:
        copy.start()

    def peer(k):
        bits = range((n - 1).bit_length())
        return sum((me // 2**b + k // 2**b) % 2 * 2**b for b in bits)

    barrier = pltpu.get_barrier_semaphore()
    for k in range(1, n):
        pl.semaphore_signal(
            barrier,
            inc=1,
            device_id={"chan": peer(k)},
            device_id_type=pl.DeviceIdType.MESH,
        )
    own_raw.start()
    copy_table.start()
    copy_phase.start()
    for copy in small:
        copy.wait()
    lane = lax.broadcasted_iota(jnp.int32, metas.shape[1:], 1)
    meta = jnp.full(metas.shape[1:], count_ref[0], jnp.int32)
    for c in range(nchan):
        for w in range(nwin):
            meta = jnp.where(lane == c * nwin + w, valid_ref[c, w], meta)
    for row in range(2 * nchan * nchan):
        meta = jnp.where(lane == nchan * nwin + row, bin_ref[row], meta)
    meta_ref[...] = meta
    pl.semaphore_wait(barrier, n - 1)
    own_meta.start()

    def remote(src, dst, send, recv, target):
        return pltpu.make_async_remote_copy(
            src_ref=src,
            dst_ref=dst,
            send_sem=send,
            recv_sem=recv,
            device_id={"chan": target},
            device_id_type=pl.DeviceIdType.MESH,
        )

    def meta_copy(k, source):
        return remote(
            meta_ref, metas.at[source], send_m.at[k], recv_m.at[k], peer(k)
        )

    def raw_copy(k, source):
        target = peer(k)
        return remote(
            spectra_ref.at[:, :, :, mine(target)], raw.at[source], send_a.at[k], recv_a.at[k], target
        )

    order = range(n - 1, 0, -1)
    for k in order:
        meta_copy(k, me).start()
    for k in order:
        raw_copy(k, me).start()

    own_meta.wait()
    for k in range(1, n):
        meta_copy(k, peer(k)).wait_recv()
    values = metas[:, 0, :]
    lane = lax.broadcasted_iota(jnp.int32, (n, LANES), 1)
    nvalid = nchan * nwin
    npairs = 2 * nchan * nchan
    is_count = lane == nvalid + npairs
    count = jnp.sum(jnp.where(is_count, values, 0), axis=1, keepdims=True)
    is_pair = (lane >= nvalid) & (lane < nvalid + npairs)
    dropped = is_pair & ((lane - nvalid >= count) | (values < 0))
    values = jnp.where(dropped, -1, jnp.where(is_count, 0, values))
    spread = jnp.dot(
        values.astype(jnp.float32).astype(jnp.bfloat16),
        expand_ref[...],
        preferred_element_type=jnp.float32,
    )
    self_bin = spread[:, :LANES]
    cross_bin = spread[:, LANES : 2 * LANES]
    first_ok = spread[:, 2 * LANES : 3 * LANES] > 0.5
    second_valid = spread[:, 3 * LANES :]
    self_bin = jnp.where(first_ok & (second_valid > 0.5), self_bin, -1.0)
    cross_bin = jnp.where(first_ok, cross_bin, -1.0)
    for p in range(n):
        kept[p, 0:1, :] = self_bin[p : p + 1]
        kept[p, 1:2, :] = cross_bin[p : p + 1]
        other_valid[p, 0:1, :] = second_valid[p : p + 1]

    bin_rows = lax.broadcasted_iota(jnp.int32, (nbins, LANES), 0).astype(jnp.float32)

    def select(p, carry):
        other = other_valid[partner_ref[p], 0:1, :]
        crossing = jnp.where(other > 0.5, kept[p, 1:2, :], -1.0)
        at = pl.multiple_of(p * LANES, LANES)
        own = kept[p, 0:1, :]
        self_selector[p] = jnp.where(bin_rows == own, 1.0, 0.0).astype(jnp.bfloat16)
        selector[:, pl.ds(at, LANES)] = jnp.where(bin_rows == crossing, 1.0, 0.0).astype(
            jnp.bfloat16
        )
        return carry

    lax.fori_loop(0, n, select, 0)

    def prepare(p):
        x = raw[p].astype(jnp.float32).reshape(nchan, 2 * nwin, nfreq)
        swapped, even = swap_pairs(x)
        power = x * x + swapped * swapped
        scales = []
        for b in range(nfreq // BAND):
            total = jnp.sum(power[:, :, b * BAND : (b + 1) * BAND], axis=-1, keepdims=True)
            scale = lax.rsqrt(total * (1.0 / BAND) + 1e-06)
            scales.append(jnp.broadcast_to(scale, (nchan, 2 * nwin, BAND)))
        scale = jnp.concatenate(scales, axis=-1)
        white = x * scale
        turn = jnp.where(even, -swapped, swapped) * scale
        for s in range(nchan):
            at = s * nrow
            part = jnp.concatenate([white[s:], white[:s]], axis=0) if s else white
            rolled[p, at : at + nrow, :] = part.reshape(nrow, nfreq).astype(jnp.bfloat16)
            part = jnp.concatenate([turn[s:], turn[:s]], axis=0) if s else turn
            turned[p, at : at + nrow, :] = part.reshape(nrow, nfreq).astype(jnp.bfloat16)

    def multiply_self(p, slot):
        x = rolled[p, 0:nrow, :]
        for s in range(nchan):
            here = slice(s * nrow, (s + 1) * nrow)
            rows = slice(slot * LANES + s * nrow, slot * LANES + (s + 1) * nrow)
            self_products[rows, 0:nfreq] = x * rolled[p, here, :]
            self_products[rows, nfreq : 2 * nfreq] = x * turned[p, here, :]

    totals[...] = jnp.zeros_like(totals)

    def add_group(members):
        for slot, p in enumerate(members):
            multiply_self(p, slot)
            spread_selector[:, slot * LANES : (slot + 1) * LANES] = self_selector[p]
        totals[...] += jnp.dot(
            spread_selector[...], self_products[...], preferred_element_type=jnp.float32
        )

    arrival = list(range(n // 2)) + list(range(n - 1, n // 2 - 1, -1))
    for g in range(0, n, GROUP):
        members = [peer(k) for k in arrival[g : g + GROUP]]
        for k, source in zip(arrival[g : g + GROUP], members):
            if k == 0:
                own_raw.wait()
            else:
                raw_copy(k, source).wait_recv()
            prepare(source)
        add_group(members)

    def multiply(p):
        q = partner_ref[p]
        x = rolled[p, 0:nrow, :]
        at = pl.multiple_of(p * LANES, LANES)
        for s in range(nchan):
            here = slice(s * nrow, (s + 1) * nrow)
            mid = at + s * nrow
            products[pl.ds(mid, nrow), 0:nfreq] = x * rolled[q, here, :]
            products[pl.ds(mid, nrow), nfreq : 2 * nfreq] = x * turned[q, here, :]

    def multiply_four(i, carry):
        for j in range(4):
            multiply(4 * i + j)
        return carry

    lax.fori_loop(0, n // 4, multiply_four, 0)

    terms = totals[...] + jnp.dot(
        selector[...], products[...], preferred_element_type=jnp.float32
    )
    outgoing[...] = terms.reshape(n, nbins_dev, 2 * nfreq).astype(jnp.bfloat16)

    def term_copy(k, source):
        target = peer(k)
        return remote(
            outgoing.at[target], incoming.at[source], send_b.at[k], recv_b.at[k], target
        )

    own_terms = pltpu.make_async_copy(outgoing.at[me], incoming.at[me], local_sems.at[4])
    for k in order:
        term_copy(k, me).start()
    own_terms.start()
    copy_table.wait()
    copy_phase.wait()
    own_terms.wait()
    for k in range(1, n):
        term_copy(k, peer(k)).wait_recv()

    stacked = incoming[...].astype(jnp.float32).reshape(nbins, 2 * nfreq).astype(jnp.bfloat16)
    lags = jnp.dot(stacked, table[...], preferred_element_type=jnp.float32)
    lags = jnp.sum(lags.reshape(n, nbins_dev, 2 * LAGS) * phases[...], axis=0)
    out_ref[...] = lags[:, :LAGS] + lags[:, LAGS:]

    for k in range(1, n):
        meta_copy(k, me).wait_send()
        raw_copy(k, me).wait_send()
        term_copy(k, me).wait_send()


def on_device_slices(spectra, valid, partner, pair_bin, pair_count):
    n = lax.axis_size("chan")
    nchan, nwin, _, nfreq_all = spectra.shape
    nfreq = nfreq_all // n
    nrow = nchan * nwin * 2
    nbins = n * BINS_DEV
    scale = 1.0 / (math.sqrt(nfreq_all) * nwin * math.sqrt(PAIRS_DEV // BINS_DEV))
    hbm = pl.BlockSpec(memory_space=pltpu.HBM)
    vmem = pl.BlockSpec(memory_space=pltpu.VMEM)
    dma = pltpu.SemaphoreType.DMA
    return pl.pallas_call(
        functools.partial(kernel, (n, nchan, nwin, nfreq, BINS_DEV)),
        out_shape=jax.ShapeDtypeStruct((BINS_DEV, LAGS), jnp.float32),
        in_specs=[hbm] * 8,
        out_specs=vmem,
        scratch_shapes=[
            pltpu.SMEM(valid.shape, jnp.int32),
            pltpu.SMEM(partner.shape, jnp.int32),
            pltpu.SMEM(pair_bin.shape, jnp.int32),
            pltpu.SMEM(pair_count.shape, jnp.int32),
            pltpu.VMEM((LANES, 4 * LANES), jnp.bfloat16),
            pltpu.VMEM((1, LANES), jnp.int32),
            pltpu.VMEM((n, nchan, nwin, 2, nfreq), jnp.bfloat16),
            pltpu.VMEM((n, 1, LANES), jnp.int32),
            pltpu.VMEM((2 * nfreq, 2 * LAGS), jnp.bfloat16),
            pltpu.VMEM((n, 1, 2 * LAGS), jnp.float32),
            pltpu.VMEM((n, nchan * nrow, nfreq), jnp.bfloat16),
            pltpu.VMEM((n, nchan * nrow, nfreq), jnp.bfloat16),
            pltpu.VMEM((n, 8, LANES), jnp.float32),
            pltpu.VMEM((n, 8, LANES), jnp.float32),
            pltpu.VMEM((nbins, n * LANES), jnp.bfloat16),
            pltpu.VMEM((n * LANES, 2 * nfreq), jnp.bfloat16),
            pltpu.VMEM((n, nbins, LANES), jnp.bfloat16),
            pltpu.VMEM((nbins, GROUP * LANES), jnp.bfloat16),
            pltpu.VMEM((GROUP * LANES, 2 * nfreq), jnp.bfloat16),
            pltpu.VMEM((nbins, 2 * nfreq), jnp.float32),
            pltpu.VMEM((n, BINS_DEV, 2 * nfreq), jnp.bfloat16),
            pltpu.VMEM((n, BINS_DEV, 2 * nfreq), jnp.bfloat16),
            dma((10,)),
            dma((n,)),
            dma((n,)),
            dma((n,)),
            dma((n,)),
            dma((n,)),
            dma((n,)),
        ],
        compiler_params=pltpu.CompilerParams(
            collective_id=0, has_side_effects=True, vmem_limit_bytes=60 * 1024 * 1024
        ),
    )(
        spectra,
        valid,
        partner,
        pair_bin,
        pair_count,
        jnp.asarray(expanders(nchan, nwin)),
        jnp.asarray(base_table(nfreq)),
        jnp.asarray(slice_phases(n, nfreq, scale)),
    )


def solution(mesh):
    in_specs = (
        P(("grp", "chan"), None, None, None),
        P(("grp", "chan"), None),
        P(),
        P(("grp", "chan")),
        P(("grp", "chan")),
    )
    out_specs = P(("grp", "chan"), None)
    whole_bands = F % (mesh.shape["chan"] * BAND) == 0
    return jax.shard_map(
        on_device_slices if whole_bands else on_device_blocks,
        mesh=mesh,
        in_specs=in_specs,
        out_specs=out_specs,
        check_vma=False,
    )
```

profile of v0, /device:TPU:0, one launch (start us, length us, event | category | flops | bytes accessed | tf_op | source)
XLA Modules:
  0.0 23.8 jit_solution(1716320190295659128)
XLA Ops:
  0.7 21.8 %shard_map.82 = f32[8,1024]{1,0:T(8,128)} custom-call(bf16[4,4,2,4096]{3,2,1,0:T(2,128)(2,1)} %spectra_ref.1, s32[4,4]{1,0:T(4,128)} %valid_hbm.1, s32[16]{0:T(128)} %partner_hbm.1, s32[32]{0:T(128)} %bin_hbm.1, s32[1]{0:T(128)S(6)} %copy.10.count_hbm, bf16[128,512]{1,0:T(8,128)(2,1)} %constant.6.clone.expand_hbm, ...), custom_call_target="tpu_custom_call" | custom-call | tf_op jit(solution)/shard_map/pallas_call | solution.py:425
  22.4 1.4 %copy.11 = f32[8,1024]{1,0:T(8,128)} copy(f32[8,1024]{1,0:T(8,128)} %shard_map.82) | data formatting | bytes 65536
where the time goes:
time: 24 us; the launch traced here: 23.8 us
  Pallas kernels  21.8 us (91%)
  local copies, waits for them, and re-layouts  1.38 us (6%)
  between operations  0.66 us (3%)
    pallas_call x1, Pallas kernels, on_device_slices(): pl.pallas_call(functools.partial(kernel, (n, nchan, nwin, nfreq, BINS_DEV...  21.8 us
    unnamed x1, local copies, waits for them, and re-layouts  1.38 us

commit v1 on v0

--- a/solution.py
+++ b/solution.py
@@ -257,24 +257,29 @@
 
     def meta_copy(k, source):
         return remote(
-            meta_ref, metas.at[source], send_m.at[k], recv_m.at[k], peer(k)
+            meta_ref, metas.at[source], send_m, recv_m, peer(k)
         )
 
     def raw_copy(k, source):
         target = peer(k)
         return remote(
-            spectra_ref.at[:, :, :, mine(target)], raw.at[source], send_a.at[k], recv_a.at[k], target
-        )
+            spectra_ref.at[:, :, :, mine(target)], raw.at[source], send_a, recv_a.at[group_of[k]], target
+        )
+
+    def span(buffer, count, send, recv):
+        part = buffer.at[pl.ds(0, count)]
+        return remote(part, part, send, recv, peer(1))
 
     order = range(n - 1, 0, -1)
+    arrival = list(range(n // 2)) + list(range(n - 1, n // 2 - 1, -1))
+    group_of = {k: i // GROUP for i, k in enumerate(arrival)}
     for k in order:
         meta_copy(k, me).start()
     for k in order:
         raw_copy(k, me).start()
 
     own_meta.wait()
-    for k in range(1, n):
-        meta_copy(k, peer(k)).wait_recv()
+    span(metas, n - 1, send_m, recv_m).wait_recv()
     values = metas[:, 0, :]
     lane = lax.broadcasted_iota(jnp.int32, (n, LANES), 1)
     nvalid = nchan * nwin
@@ -352,14 +357,15 @@
             spread_selector[...], self_products[...], preferred_element_type=jnp.float32
         )
 
-    arrival = list(range(n // 2)) + list(range(n - 1, n // 2 - 1, -1))
     for g in range(0, n, GROUP):
-        members = [peer(k) for k in arrival[g : g + GROUP]]
-        for k, source in zip(arrival[g : g + GROUP], members):
-            if k == 0:
-                own_raw.wait()
-            else:
-                raw_copy(k, source).wait_recv()
+        ks = arrival[g : g + GROUP]
+        members = [peer(k) for k in ks]
+        if 0 in ks:
+            own_raw.wait()
+        remote_count = sum(k != 0 for k in ks)
+        if remote_count:
+            span(raw, remote_count, send_a, recv_a.at[g // GROUP]).wait_recv()
+        for source in members:
             prepare(source)
         add_group(members)
 
@@ -388,7 +394,7 @@
     def term_copy(k, source):
         target = peer(k)
         return remote(
-            outgoing.at[target], incoming.at[source], send_b.at[k], recv_b.at[k], target
+            outgoing.at[target], incoming.at[source], send_b, recv_b, target
         )
 
     own_terms = pltpu.make_async_copy(outgoing.at[me], incoming.at[me], local_sems.at[4])
@@ -398,18 +404,16 @@
     copy_table.wait()
     copy_phase.wait()
     own_terms.wait()
-    for k in range(1, n):
-        term_copy(k, peer(k)).wait_recv()
+    span(incoming, n - 1, send_b, recv_b).wait_recv()
 
     stacked = incoming[...].astype(jnp.float32).reshape(nbins, 2 * nfreq).astype(jnp.bfloat16)
     lags = jnp.dot(stacked, table[...], preferred_element_type=jnp.float32)
     lags = jnp.sum(lags.reshape(n, nbins_dev, 2 * LAGS) * phases[...], axis=0)
     out_ref[...] = lags[:, :LAGS] + lags[:, LAGS:]
 
-    for k in range(1, n):
-        meta_copy(k, me).wait_send()
-        raw_copy(k, me).wait_send()
-        term_copy(k, me).wait_send()
+    span(metas, n - 1, send_m, recv_m).wait_send()
+    span(raw, n - 1, send_a, recv_a.at[0]).wait_send()
+    span(incoming, n - 1, send_b, recv_b).wait_send()
 
 
 def on_device_slices(spectra, valid, partner, pair_bin, pair_count):
@@ -424,7 +428,7 @@
     dma = pltpu.SemaphoreType.DMA
     return pl.pallas_call(
         functools.partial(kernel, (n, nchan, nwin, nfreq, BINS_DEV)),
-        out_shape=jax.ShapeDtypeStruct((BINS_DEV, LAGS), jnp.float32),
+        out_shape=pltpu.VMEM((BINS_DEV, LAGS), jnp.float32),
         in_specs=[hbm] * 8,
         out_specs=vmem,
         scratch_shapes=[
@@ -451,12 +455,12 @@
             pltpu.VMEM((n, BINS_DEV, 2 * nfreq), jnp.bfloat16),
             pltpu.VMEM((n, BINS_DEV, 2 * nfreq), jnp.bfloat16),
             dma((10,)),
-            dma((n,)),
-            dma((n,)),
-            dma((n,)),
-            dma((n,)),
-            dma((n,)),
-            dma((n,)),
+            dma,
+            dma((n // GROUP,)),
+            dma,
+            dma,
+            dma,
+            dma,
         ],
         compiler_params=pltpu.CompilerParams(
             collective_id=0, has_side_effects=True, vmem_limit_bytes=60 * 1024 * 1024

time: 24 us -> 21.4 us (0.89)
  Pallas kernels: 21.8 us -> 20 us
  local copies, waits for them, and re-layouts: 1.38 us -> 0.62 us
    pallas_call x1, Pallas kernels: 21.8 us -> 20 us  [on_device_slices(): pl.pallas_call(functools.partial(kernel, (n, nchan, nwin, nfreq, BINS_DEV...]
    unnamed x1, local copies, waits for them, and re-layouts: 1.38 us -> 0.62 us
where the time goes in v1:
time: 21.4 us; the launch traced here: 21.3 us
  Pallas kernels  20 us (93%)
  between operations  0.66 us (3%)
  local copies, waits for them, and re-layouts  0.62 us (3%)
    pallas_call x1, Pallas kernels, on_device_slices(): pl.pallas_call(functools.partial(kernel, (n, nchan, nwin, nfreq, BINS_DEV...  20 us
    unnamed x1, local copies, waits for them, and re-layouts  0.62 us

profile of v1, /device:TPU:0, one launch (start us, length us, event | category | flops | bytes accessed | tf_op | source)
XLA Modules:
  0.0 21.3 jit_solution(3232319658866979421)
XLA Ops:
  0.7 20.0 %shard_map.82 = f32[8,1024]{1,0:T(8,128)S(1)} custom-call(bf16[4,4,2,4096]{3,2,1,0:T(2,128)(2,1)} %spectra_ref.1, s32[4,4]{1,0:T(4,128)} %valid_hbm.1, s32[16]{0:T(128)} %partner_hbm.1, s32[32]{0:T(128)} %bin_hbm.1, s32[1]{0:T(128)S(6)} %copy.11.count_hbm, bf16[128,512]{1,0:T(8,128)(2,1)} %constant.6.clone.expand_hbm, ...), custom_call_target="tpu_custom_call" | custom-call | tf_op jit(solution)/shard_map/pallas_call | solution.py:429
  20.7 0.6 %copy.10 = f32[8,1024]{1,0:T(8,128)} copy(f32[8,1024]{1,0:T(8,128)S(1)} %shard_map.82) | data formatting | bytes 65536

commit v2 on v1

v2 whole, which is shorter than its diff:
```python
import functools
import math

import jax
import jax.numpy as jnp
import ml_dtypes
import numpy as np
from jax import lax
from jax.experimental import pallas as pl
from jax.experimental.pallas import tpu as pltpu
from jax.sharding import PartitionSpec as P

F = 4096
BAND = 128
LAGS = 1024
BINS_DEV = 8
PAIRS_DEV = 32
LANES = 128
GROUP = 4
PLANE = 4


def from_partner(block, axis, bit):
    count = lax.axis_size(axis)
    route = []
    for low in range(count):
        high = low | 1 << bit
        if high != low and high < count:
            route += [(low, high), (high, low)]
    return lax.ppermute(block, axis, route)


def whiten(spectra, valid):
    values = spectra.astype(jnp.float32)
    power = values[:, :, 0] * values[:, :, 0] + values[:, :, 1] * values[:, :, 1]
    nchan, nwin, nfreq = power.shape
    banded = jnp.mean(power.reshape(nchan, nwin, nfreq // BAND, BAND), axis=-1)
    amplitude = jnp.repeat(jnp.sqrt(banded + 1e-06), BAND, axis=-1)
    weights = valid.astype(jnp.float32)[:, :, None, None]
    return (values * weights / amplitude[:, :, None, :]).astype(jnp.bfloat16)


def lag_table():
    freqs = jnp.arange(F, dtype=jnp.int32)
    shifts = jnp.arange(LAGS, dtype=jnp.int32) - LAGS // 2
    phase = jnp.mod(freqs[:, None] * shifts[None, :], 2 * F)
    angle = phase.astype(jnp.float32) * (2.0 * math.pi / (2 * F))
    scale = 1.0 / math.sqrt(F)
    return jnp.concatenate([jnp.cos(angle) * scale, -jnp.sin(angle) * scale], axis=0).astype(
        jnp.bfloat16
    )


def cross_product(left_part, right_part):
    return jnp.einsum("awf,bwf->abf", left_part, right_part, preferred_element_type=jnp.float32)


def correlate(own_block, other_block, table):
    own_real = own_block[:, :, 0]
    own_imag = own_block[:, :, 1]
    oth_real = other_block[:, :, 0]
    oth_imag = other_block[:, :, 1]
    real_part = cross_product(own_real, oth_real) + cross_product(own_imag, oth_imag)
    imag_part = cross_product(own_imag, oth_real) - cross_product(own_real, oth_imag)
    nchan = own_block.shape[0]
    nwin = own_block.shape[1]
    spec = (jnp.concatenate([real_part, imag_part], axis=-1) * (1.0 / nwin)).reshape(
        nchan * nchan, -1
    )
    spec = spec.astype(jnp.bfloat16)
    return jnp.dot(spec, table, preferred_element_type=jnp.float32)


def select_sum(selector, corr_high, corr_low):
    return jnp.dot(selector, corr_high, preferred_element_type=jnp.float32) + jnp.dot(
        selector, corr_low, preferred_element_type=jnp.float32
    )


def on_device_blocks(spectra, valid, partner, pair_bin, pair_count):
    white = whiten(spectra, valid)
    nblocks = lax.axis_size("chan")
    round_mask = partner[0]
    paired = white
    for bit_index in range(nblocks.bit_length() - 1):
        swapped = from_partner(paired, "chan", bit_index)
        paired = jnp.where(round_mask >> bit_index & 1 == 1, swapped, paired)
    table = lag_table()
    self_corr = correlate(white, white, table)
    cross_corr = correlate(white, paired, table)
    corr = jnp.concatenate([self_corr, cross_corr], axis=0)
    corr_high = corr.astype(jnp.bfloat16)
    corr_low = (corr - corr_high.astype(jnp.float32)).astype(jnp.bfloat16)
    rows = jnp.arange(corr.shape[0], dtype=jnp.int32)
    live_rows = (rows < pair_count[0]) & (pair_bin >= 0)
    kept_bins = jnp.where(live_rows, pair_bin, -1)
    targets = lax.iota(jnp.int32, nblocks * BINS_DEV)
    selector = (kept_bins[None, :] == targets[:, None]).astype(jnp.bfloat16)
    terms = select_sum(selector, corr_high, corr_low).reshape(nblocks, BINS_DEV, -1)
    received = lax.all_to_all(terms, "chan", split_axis=0, concat_axis=0, tiled=True)
    summed = jnp.sum(received, axis=0)
    return summed * (1.0 / math.sqrt(PAIRS_DEV // BINS_DEV))


def base_table(nfreq):
    shifts = np.arange(LAGS) - LAGS // 2
    angle = np.mod(np.arange(nfreq)[:, None] * shifts[None, :], 2 * F) * (2.0 * math.pi / (2 * F))
    cos, sin = np.cos(angle), np.sin(angle)
    return np.concatenate(
        [np.concatenate([cos, sin], axis=1), np.concatenate([-sin, cos], axis=1)], axis=0
    ).astype(ml_dtypes.bfloat16)


def slice_phases(nslices, nfreq, scale):
    shifts = np.arange(LAGS) - LAGS // 2
    first = np.arange(nslices) * nfreq
    angle = np.mod(first[:, None] * shifts[None, :], 2 * F) * (2.0 * math.pi / (2 * F))
    both = np.concatenate([np.cos(angle), -np.sin(angle)], axis=1) * scale
    return both.astype(np.float32)[:, None, :]


def expanders(nchan, nwin):
    row = np.arange(LANES)
    per_chan = 2 * nwin
    chan = row // per_chan % nchan
    shift = row // (per_chan * nchan)
    npairs = nchan * nchan

    def pair(step):
        return chan * nchan + (chan + step) % nchan

    def reverse(step):
        return (chan + step) % nchan * nchan + chan

    lanes = (
        pair(0),
        pair(1),
        reverse(1),
        pair(2),
        npairs + pair(shift),
        npairs + reverse(shift),
    )
    return np.concatenate(
        [(np.arange(LANES)[:, None] == lane[None, :]) for lane in lanes], axis=1
    ).astype(ml_dtypes.bfloat16)


def swap_pairs(rows):
    size = rows.shape[-2]
    axis = rows.ndim - 2
    even = lax.broadcasted_iota(jnp.int32, rows.shape, axis) % 2 == 0
    return jnp.where(
        even, pltpu.roll(rows, size - 1, axis), pltpu.roll(rows, 1, axis)
    ), even


def halves_swapped(rows):
    half = rows.shape[0] // 2
    return jnp.concatenate([rows[half:], rows[:half]], axis=0)


def kernel(
    dims,
    spectra_hbm,
    valid_hbm,
    partner_hbm,
    bin_hbm,
    count_hbm,
    expand_hbm,
    table_hbm,
    phase_hbm,
    out_ref,
    own,
    valid_ref,
    partner_ref,
    bin_ref,
    count_ref,
    expand_ref,
    meta_ref,
    metas,
    white,
    plain,
    odd,
    plain_turn,
    odd_turn,
    table,
    phases,
    cross_bins,
    select_re,
    select_im,
    last_re,
    last_im,
    products,
    last_products,
    total_re,
    total_im,
    outgoing,
    incoming,
    local_sems,
    send_a,
    recv_a,
    send_m,
    recv_m,
    send_b,
    recv_b,
    ready,
    token,
):
    n, nchan, nwin, nfreq, nbins_dev = dims
    nrow = nchan * nwin * 2
    nbins = n * nbins_dev
    npairs = nchan * nchan
    ngroups = n // GROUP
    me = lax.axis_index("chan")

    def peer(k):
        bits = range((n - 1).bit_length())
        return sum((me // 2**b + k // 2**b) % 2 * 2**b for b in bits)

    def remote(src, dst, send, recv, target):
        return pltpu.make_async_remote_copy(
            src_ref=src,
            dst_ref=dst,
            send_sem=send,
            recv_sem=recv,
            device_id={"chan": target},
            device_id_type=pl.DeviceIdType.MESH,
        )

    def span(buffer, first, count, send, recv):
        part = buffer.at[pl.ds(first, count)]
        return remote(part, part, send, recv, peer(1))

    copy_own = pltpu.make_async_copy(spectra_hbm, own, local_sems.at[0])
    copy_table = pltpu.make_async_copy(table_hbm, table, local_sems.at[1])
    copy_phase = pltpu.make_async_copy(phase_hbm, phases, local_sems.at[2])
    small = [
        pltpu.make_async_copy(src, dst, local_sems.at[3 + i])
        for i, (src, dst) in enumerate(
            (
                (valid_hbm, valid_ref),
                (bin_hbm, bin_ref),
                (count_hbm, count_ref),
                (partner_hbm, partner_ref),
                (expand_hbm, expand_ref),
            )
        )
    ]
    copy_own.start()
    for copy in small[:3]:
        copy.start()
    plane = me // PLANE
    is_last = plane == n // PLANE - 1
    barrier = pltpu.get_barrier_semaphore()

    def signal(sem, ks):
        for k in ks:
            pl.semaphore_signal(
                sem,
                inc=1,
                device_id={"chan": peer(k)},
                device_id_type=pl.DeviceIdType.MESH,
            )

    @pl.when(jnp.logical_not(is_last))
    def _():
        signal(barrier, range(n - 1, 0, -1))

    for copy in small[3:]:
        copy.start()
    copy_table.start()
    copy_phase.start()
    for copy in small[:3]:
        copy.wait()

    lane = lax.broadcasted_iota(jnp.int32, meta_ref.shape, 1)
    bins = jnp.full(meta_ref.shape, -1, jnp.int32)
    for row in range(2 * npairs):
        bins = jnp.where(lane == row, bin_ref[row], bins)
    bins = jnp.where((lane < count_ref[0]) & (bins >= 0), bins, -1)
    meta_ref[...] = bins

    sub = lax.broadcasted_iota(jnp.int32, (nchan, 2 * nwin, LANES), 1) // 2
    chan = lax.broadcasted_iota(jnp.int32, (nchan, 2 * nwin, LANES), 0)
    usable = jnp.zeros((nchan, 2 * nwin, LANES), jnp.float32)
    for c in range(nchan):
        for w in range(nwin):
            usable = jnp.where(
                (chan == c) & (sub == w), valid_ref[c, w].astype(jnp.float32), usable
            )

    def whiten_slice(t):
        here = pl.ds(pl.multiple_of(t * nfreq, nfreq), nfreq)
        x = own[:, :, :, here].astype(jnp.float32)
        x = x.reshape(nchan, 2 * nwin, nfreq)
        swapped, _ = swap_pairs(x)
        power = x * x + swapped * swapped
        for b in range(nfreq // BAND):
            band = slice(b * BAND, (b + 1) * BAND)
            total = jnp.sum(power[:, :, band], axis=-1, keepdims=True)
            scale = lax.rsqrt(total * (1.0 / BAND) + 1e-06) * usable
            rows = (x[:, :, band] * scale).reshape(nrow, BAND)
            white[t, :, band] = rows.astype(jnp.bfloat16)

    def send_meta(k):
        remote(meta_ref, metas.at[k], send_m, recv_m, peer(k)).start()

    def send_white(k):
        remote(white.at[peer(k)], plain.at[k], send_a, recv_a.at[k // GROUP], peer(k)).start()

    def each(act, ks):
        for k in ks:
            act(k)

    near = [7, 6, 5, 4]
    middle = [11, 10, 9, 8]
    far = [15, 14, 13, 12]
    inside = [3, 2, 1]
    copy_own.wait()

    @pl.when(jnp.logical_not(is_last))
    def _():
        def step(i, carry):
            for u in range(4):
                whiten_slice(4 * i + u)
            return carry

        lax.fori_loop(0, n // 4, step, 0)
        pl.semaphore_wait(barrier, 3 * PLANE - 1)

    @pl.when(is_last)
    def _():
        pl.semaphore_wait(barrier, 3 * PLANE)
        signal(ready, far + middle + near)
        each(send_meta, far + middle + near)
        for k in far + middle + near:
            whiten_slice(peer(k))
            send_white(k)
        for k in [*inside, 0]:
            whiten_slice(peer(k))
        pl.semaphore_wait(token, 1)
        each(send_meta, inside)
        each(send_white, inside)

    @pl.when(plane == 2)
    def _():
        each(send_meta, far + middle + inside)
        each(send_white, far + middle)
        pl.semaphore_wait(ready, PLANE)
        signal(token, near[-1:])
        each(send_meta, near)
        each(send_white, near + inside)

    @pl.when(plane == 1)
    def _():
        each(send_meta, far + near + inside)
        each(send_white, far + near)
        pl.semaphore_wait(ready, PLANE)
        each(send_meta, middle)
        each(send_white, middle + inside)

    @pl.when(plane == 0)
    def _():
        each(send_meta, middle + near + inside)
        each(send_white, middle)
        pl.semaphore_wait(ready, PLANE)
        each(send_meta, far)
        each(send_white, far + near + inside)

    order = range(n - 1, 0, -1)

    plain[0] = white[me]
    metas[0] = meta_ref[...]
    for copy in small[3:]:
        copy.wait()
    mirror = partner_ref[0]
    firsts = []
    for j in range(n // 2):
        first = j
        for b in reversed(range((n - 1).bit_length())):
            spread = j // 2**b * 2 ** (b + 1) + j % 2**b
            first = jnp.where((mirror >> b) % 2 == 1, spread, first)
        firsts.append(first)

    def prepare(k):
        x = plain[k].astype(jnp.float32)
        swapped, even = swap_pairs(x)
        turn = jnp.where(even, -swapped, swapped)
        step = 2 * nwin
        odd[k] = jnp.concatenate([x[step:], x[:step]], axis=0).astype(jnp.bfloat16)
        plain_turn[k] = turn.astype(jnp.bfloat16)
        odd_turn[k] = jnp.concatenate([turn[step:], turn[:step]], axis=0).astype(jnp.bfloat16)

    def put(target, at, left, right, right_turn):
        target[pl.ds(at, nrow), 0:nfreq] = left * right
        target[pl.ds(at, nrow), nfreq : 2 * nfreq] = left * right_turn

    def multiply_self(target, g):
        for u in range(GROUP):
            k = g * GROUP + u
            x = plain[k]
            xt = plain_turn[k]
            put(target, u * nrow, x, x, xt)
            put(target, LANES + u * nrow, x, odd[k], odd_turn[k])
            put(target, 2 * LANES + u * nrow, x, halves_swapped(x), halves_swapped(xt))

    span(metas, 1, n - 1, send_m, recv_m).wait_recv()
    spread = jnp.dot(
        metas[:, 0, :].astype(jnp.float32).astype(jnp.bfloat16),
        expand_ref[...],
        preferred_element_type=jnp.float32,
    )
    for k in range(n):
        cross_bins[k, 0:1, :] = spread[k : k + 1, 4 * LANES : 5 * LANES]
        cross_bins[k, 1:2, :] = spread[k : k + 1, 5 * LANES : 6 * LANES]
    self_bins = spread[:, : 4 * LANES]
    slot = lax.broadcasted_iota(jnp.int32, self_bins.shape, 0) % GROUP
    place = lax.broadcasted_iota(jnp.int32, self_bins.shape, 1) % LANES // nrow
    self_bins = jnp.where(slot == place, self_bins, 0.0)
    bin_rows = lax.broadcasted_iota(jnp.int32, (nbins, LANES), 0).astype(jnp.float32)

    def one_hot(row):
        return jnp.where(bin_rows == row, 1.0, 0.0)

    for g in range(ngroups):
        row = jnp.sum(self_bins[g * GROUP : (g + 1) * GROUP], axis=0, keepdims=True)
        same, ahead, back, across = [
            one_hot(row[:, i * LANES : (i + 1) * LANES]) for i in range(4)
        ]
        final = g == ngroups - 1
        for target, middle in (
            (last_re if final else select_re.at[g], ahead + back),
            (last_im if final else select_im.at[g], ahead - back),
        ):
            target[:, 0:LANES] = same.astype(jnp.bfloat16)
            target[:, LANES : 2 * LANES] = middle.astype(jnp.bfloat16)
            target[:, 2 * LANES : 3 * LANES] = across.astype(jnp.bfloat16)
    base = 3 * LANES
    for j in range(n // 2):
        ahead = one_hot(cross_bins[firsts[j], 0:1, :])
        back = one_hot(cross_bins[firsts[j] ^ mirror, 1:2, :])
        here = slice(base + j * LANES, base + (j + 1) * LANES)
        last_re[:, here] = (ahead + back).astype(jnp.bfloat16)
        last_im[:, here] = (ahead - back).astype(jnp.bfloat16)

    def product(left, right):
        return jnp.dot(left, right, preferred_element_type=jnp.float32)

    for g in range(ngroups):
        here = range(max(g * GROUP, 1), (g + 1) * GROUP)
        span(plain, here[0], len(here), send_a, recv_a.at[g]).wait_recv()
        for k in range(g * GROUP, (g + 1) * GROUP):
            prepare(k)
        if g < ngroups - 1:
            multiply_self(products, g)
            part_re = product(select_re[g], products[:, 0:nfreq])
            part_im = product(select_im[g], products[:, nfreq : 2 * nfreq])
            total_re[...] = part_re if g == 0 else total_re[...] + part_re
            total_im[...] = part_im if g == 0 else total_im[...] + part_im
        else:
            multiply_self(last_products, g)

    for j in range(n // 2):
        x = plain[firsts[j]]
        q = firsts[j] ^ mirror
        at = base + j * LANES
        y, yt, z, zt = plain[q], plain_turn[q], odd[q], odd_turn[q]
        put(last_products, at, x, y, yt)
        put(last_products, at + nrow, x, z, zt)
        put(last_products, at + 2 * nrow, x, halves_swapped(y), halves_swapped(yt))
        put(last_products, at + 3 * nrow, x, halves_swapped(z), halves_swapped(zt))

    terms_re = total_re[...] + product(last_re[...], last_products[:, 0:nfreq])
    outgoing[:, :, 0:nfreq] = terms_re.reshape(n, nbins_dev, nfreq).astype(jnp.bfloat16)
    terms_im = total_im[...] + product(last_im[...], last_products[:, nfreq : 2 * nfreq])
    outgoing[:, :, nfreq : 2 * nfreq] = terms_im.reshape(n, nbins_dev, nfreq).astype(jnp.bfloat16)

    for k in order:
        remote(outgoing.at[peer(k)], incoming.at[me], send_b, recv_b, peer(k)).start()
    incoming[me] = outgoing[me]
    copy_table.wait()
    copy_phase.wait()
    span(incoming, 0, n - 1, send_b, recv_b).wait_recv()

    stacked = incoming[...].astype(jnp.float32).reshape(nbins, 2 * nfreq).astype(jnp.bfloat16)
    lags = product(stacked, table[...])
    lags = jnp.sum(lags.reshape(n, nbins_dev, 2 * LAGS) * phases[...], axis=0)
    out_ref[...] = lags[:, :LAGS] + lags[:, LAGS:]

    span(metas, 1, n - 1, send_m, recv_m).wait_send()
    span(plain, 1, n - 1, send_a, recv_a.at[0]).wait_send()
    span(incoming, 0, n - 1, send_b, recv_b).wait_send()


def on_device_slices(spectra, valid, partner, pair_bin, pair_count):
    n = lax.axis_size("chan")
    nchan, nwin, _, nfreq_all = spectra.shape
    nfreq = nfreq_all // n
    nrow = nchan * nwin * 2
    nbins = n * BINS_DEV
    base = 3 * LANES
    deep = base + n // 2 * LANES
    scale = 1.0 / (math.sqrt(nfreq_all) * nwin * math.sqrt(PAIRS_DEV // BINS_DEV))
    hbm = pl.BlockSpec(memory_space=pltpu.HBM)
    vmem = pl.BlockSpec(memory_space=pltpu.VMEM)
    dma = pltpu.SemaphoreType.DMA
    bf16 = jnp.bfloat16
    return pl.pallas_call(
        functools.partial(kernel, (n, nchan, nwin, nfreq, BINS_DEV)),
        out_shape=pltpu.VMEM((BINS_DEV, LAGS), jnp.float32),
        in_specs=[hbm] * 8,
        out_specs=vmem,
        scratch_shapes=[
            pltpu.VMEM(spectra.shape, bf16),
            pltpu.SMEM(valid.shape, jnp.int32),
            pltpu.SMEM(partner.shape, jnp.int32),
            pltpu.SMEM(pair_bin.shape, jnp.int32),
            pltpu.SMEM(pair_count.shape, jnp.int32),
            pltpu.VMEM((LANES, 6 * LANES), bf16),
            pltpu.VMEM((1, LANES), jnp.int32),
            pltpu.VMEM((n, 1, LANES), jnp.int32),
            pltpu.VMEM((n, nrow, nfreq), bf16),
            pltpu.VMEM((n, nrow, nfreq), bf16),
            pltpu.VMEM((n, nrow, nfreq), bf16),
            pltpu.VMEM((n, nrow, nfreq), bf16),
            pltpu.VMEM((n, nrow, nfreq), bf16),
            pltpu.VMEM((2 * nfreq, 2 * LAGS), bf16),
            pltpu.VMEM((n, 1, 2 * LAGS), jnp.float32),
            pltpu.VMEM((n, 8, LANES), jnp.float32),
            pltpu.VMEM((n // GROUP - 1, nbins, base), bf16),
            pltpu.VMEM((n // GROUP - 1, nbins, base), bf16),
            pltpu.VMEM((nbins, deep), bf16),
            pltpu.VMEM((nbins, deep), bf16),
            pltpu.VMEM((base, 2 * nfreq), bf16),
            pltpu.VMEM((deep, 2 * nfreq), bf16),
            pltpu.VMEM((nbins, nfreq), jnp.float32),
            pltpu.VMEM((nbins, nfreq), jnp.float32),
            pltpu.VMEM((n, BINS_DEV, 2 * nfreq), bf16),
            pltpu.VMEM((n, BINS_DEV, 2 * nfreq), bf16),
            dma((8,)),
            dma,
            dma((n // GROUP,)),
            dma,
            dma,
            dma,
            dma,
            pltpu.SemaphoreType.REGULAR,
            pltpu.SemaphoreType.REGULAR,
        ],
        compiler_params=pltpu.CompilerParams(
            collective_id=0, has_side_effects=True, vmem_limit_bytes=60 * 1024 * 1024
        ),
    )(
        spectra,
        valid,
        partner,
        pair_bin,
        pair_count,
        jnp.asarray(expanders(nchan, nwin)),
        jnp.asarray(base_table(nfreq)),
        jnp.asarray(slice_phases(n, nfreq, scale)),
    )


def solution(mesh):
    in_specs = (
        P(("grp", "chan"), None, None, None),
        P(("grp", "chan"), None),
        P(),
        P(("grp", "chan")),
        P(("grp", "chan")),
    )
    out_specs = P(("grp", "chan"), None)
    whole_bands = F % (mesh.shape["chan"] * BAND) == 0
    return jax.shard_map(
        on_device_slices if whole_bands else on_device_blocks,
        mesh=mesh,
        in_specs=in_specs,
        out_specs=out_specs,
        check_vma=False,
    )
```

time: 21.4 us -> 19.8 us (0.925)
  Pallas kernels: 20 us -> 18.4 us
    pallas_call x1, Pallas kernels: 20 us -> 18.4 us  [on_device_slices(): pl.pallas_call(functools.partial(kernel, (n, nchan, nwin, nfreq, BINS_DEV...]
where the time goes in v2:
time: 19.8 us; the launch traced here: 19.7 us
  Pallas kernels  18.4 us (93%)
  between operations  0.66 us (3%)
  local copies, waits for them, and re-layouts  0.62 us (3%)
    pallas_call x1, Pallas kernels, on_device_slices(): pl.pallas_call(functools.partial(kernel, (n, nchan, nwin, nfreq, BINS_DEV...  18.4 us
    unnamed x1, local copies, waits for them, and re-layouts  0.62 us

profile of v2, /device:TPU:0, one launch (start us, length us, event | category | flops | bytes accessed | tf_op | source)
XLA Modules:
  0.0 19.7 jit_solution(7133125864763038339)
XLA Ops:
  0.7 18.4 %shard_map.82 = f32[8,1024]{1,0:T(8,128)S(1)} custom-call(bf16[4,4,2,4096]{3,2,1,0:T(2,128)(2,1)} %spectra_hbm.1, s32[4,4]{1,0:T(4,128)} %valid_hbm.1, s32[16]{0:T(128)} %partner_hbm.1, s32[32]{0:T(128)} %bin_hbm.1, s32[1]{0:T(128)S(6)} %copy.11.count_hbm, bf16[128,768]{1,0:T(8,128)(2,1)} %constant.6.clone.expand_hbm, ...), custom_call_target="tpu_custom_call" | custom-call | tf_op jit(solution)/shard_map/pallas_call | solution.py:508
  19.0 0.6 %copy.10 = f32[8,1024]{1,0:T(8,128)} copy(f32[8,1024]{1,0:T(8,128)S(1)} %shard_map.82) | data formatting | bytes 65536

commit v3 on v2

--- a/solution.py
+++ b/solution.py
@@ -180,6 +180,7 @@
     metas,
     white,
     plain,
+    same,
     odd,
     plain_turn,
     odd_turn,
@@ -188,10 +189,10 @@
     cross_bins,
     select_re,
     select_im,
-    last_re,
-    last_im,
+    cross_re,
+    cross_im,
     products,
-    last_products,
+    cross_products,
     total_re,
     total_im,
     outgoing,
@@ -211,6 +212,7 @@
     nbins = n * nbins_dev
     npairs = nchan * nchan
     ngroups = n // GROUP
+    half = n // 2
     me = lax.axis_index("chan")
 
     def peer(k):
@@ -303,7 +305,7 @@
             white[t, :, band] = rows.astype(jnp.bfloat16)
 
     def send_meta(k):
-        remote(meta_ref, metas.at[k], send_m, recv_m, peer(k)).start()
+        remote(meta_ref, metas.at[k], send_m, recv_m.at[k // half], peer(k)).start()
 
     def send_white(k):
         remote(white.at[peer(k)], plain.at[k], send_a, recv_a.at[k // GROUP], peer(k)).start()
@@ -367,22 +369,23 @@
         each(send_meta, far)
         each(send_white, far + near + inside)
 
-    order = range(n - 1, 0, -1)
-
     plain[0] = white[me]
     metas[0] = meta_ref[...]
     for copy in small[3:]:
         copy.wait()
     mirror = partner_ref[0]
-    firsts = []
-    for j in range(n // 2):
-        first = j
-        for b in reversed(range((n - 1).bit_length())):
-            spread = j // 2**b * 2 ** (b + 1) + j % 2**b
-            first = jnp.where((mirror >> b) % 2 == 1, spread, first)
-        firsts.append(first)
+    across = mirror // PLANE
+    lead = jnp.where(across == 2, 1, 0)
+    early, late = [], []
+    for j in range(PLANE):
+        inner = jnp.where(mirror == 2, j % 2, j % 2 * 2)
+        early.append(jnp.where(across == 0, j // 2 * PLANE + inner, lead * PLANE + j))
+        late.append(jnp.where(across == 0, (3 - j // 2) * PLANE + inner, 2 * PLANE + j))
+    firsts = early + late
+    sequence = [0, 1, 3, 2]
 
     def prepare(k):
+        same[k] = plain[k]
         x = plain[k].astype(jnp.float32)
         swapped, even = swap_pairs(x)
         turn = jnp.where(even, -swapped, swapped)
@@ -404,79 +407,114 @@
             put(target, LANES + u * nrow, x, odd[k], odd_turn[k])
             put(target, 2 * LANES + u * nrow, x, halves_swapped(x), halves_swapped(xt))
 
-    span(metas, 1, n - 1, send_m, recv_m).wait_recv()
-    spread = jnp.dot(
-        metas[:, 0, :].astype(jnp.float32).astype(jnp.bfloat16),
-        expand_ref[...],
-        preferred_element_type=jnp.float32,
-    )
-    for k in range(n):
-        cross_bins[k, 0:1, :] = spread[k : k + 1, 4 * LANES : 5 * LANES]
-        cross_bins[k, 1:2, :] = spread[k : k + 1, 5 * LANES : 6 * LANES]
-    self_bins = spread[:, : 4 * LANES]
-    slot = lax.broadcasted_iota(jnp.int32, self_bins.shape, 0) % GROUP
-    place = lax.broadcasted_iota(jnp.int32, self_bins.shape, 1) % LANES // nrow
-    self_bins = jnp.where(slot == place, self_bins, 0.0)
-    bin_rows = lax.broadcasted_iota(jnp.int32, (nbins, LANES), 0).astype(jnp.float32)
+    base = 3 * LANES
+
+    bin_rows = lax.broadcasted_iota(jnp.int32, (nbins, LANES), 0)
+    bin_rows = bin_rows.astype(jnp.float32).astype(jnp.bfloat16)
+    one = jnp.ones((nbins, LANES), jnp.bfloat16)
+    zero = jnp.zeros((nbins, LANES), jnp.bfloat16)
 
     def one_hot(row):
-        return jnp.where(bin_rows == row, 1.0, 0.0)
-
-    for g in range(ngroups):
-        row = jnp.sum(self_bins[g * GROUP : (g + 1) * GROUP], axis=0, keepdims=True)
-        same, ahead, back, across = [
-            one_hot(row[:, i * LANES : (i + 1) * LANES]) for i in range(4)
-        ]
-        final = g == ngroups - 1
-        for target, middle in (
-            (last_re if final else select_re.at[g], ahead + back),
-            (last_im if final else select_im.at[g], ahead - back),
-        ):
-            target[:, 0:LANES] = same.astype(jnp.bfloat16)
-            target[:, LANES : 2 * LANES] = middle.astype(jnp.bfloat16)
-            target[:, 2 * LANES : 3 * LANES] = across.astype(jnp.bfloat16)
-    base = 3 * LANES
-    for j in range(n // 2):
-        ahead = one_hot(cross_bins[firsts[j], 0:1, :])
-        back = one_hot(cross_bins[firsts[j] ^ mirror, 1:2, :])
-        here = slice(base + j * LANES, base + (j + 1) * LANES)
-        last_re[:, here] = (ahead + back).astype(jnp.bfloat16)
-        last_im[:, here] = (ahead - back).astype(jnp.bfloat16)
+        return jnp.where(bin_rows == row.astype(jnp.bfloat16), one, zero)
+
+    def select_self(part):
+        first = part * half
+        count = half - (part == 0)
+        span(metas, first + (part == 0), count, send_m, recv_m.at[part]).wait_recv()
+        spread = jnp.dot(
+            metas[first : first + half, 0, :].astype(jnp.float32).astype(jnp.bfloat16),
+            expand_ref[...],
+            preferred_element_type=jnp.float32,
+        )
+        for u in range(half):
+            cross_bins[first + u, 0:1, :] = spread[u : u + 1, 4 * LANES : 5 * LANES]
+            cross_bins[first + u, 1:2, :] = spread[u : u + 1, 5 * LANES : 6 * LANES]
+        self_bins = spread[:, : 4 * LANES]
+        slot = lax.broadcasted_iota(jnp.int32, self_bins.shape, 0) % GROUP
+        place = lax.broadcasted_iota(jnp.int32, self_bins.shape, 1) % LANES // nrow
+        self_bins = jnp.where(slot == place, self_bins, 0.0)
+        for v in range(half // GROUP):
+            i = sequence.index(part * half // GROUP + v)
+            row = jnp.sum(self_bins[v * GROUP : (v + 1) * GROUP], axis=0, keepdims=True)
+            alone, ahead, back, over = [
+                one_hot(row[:, h * LANES : (h + 1) * LANES]) for h in range(4)
+            ]
+            at = i * base
+            for target, mixed in ((select_re, ahead + back), (select_im, ahead - back)):
+                target[:, at : at + LANES] = alone
+                target[:, at + LANES : at + 2 * LANES] = mixed
+                target[:, at + 2 * LANES : at + 3 * LANES] = over
+
+    def select_cross():
+        for j in range(n // 2):
+            ahead = one_hot(cross_bins[firsts[j], 0:1, :])
+            back = one_hot(cross_bins[firsts[j] ^ mirror, 1:2, :])
+            cross_re[:, j * LANES : (j + 1) * LANES] = ahead + back
+            cross_im[:, j * LANES : (j + 1) * LANES] = ahead - back
 
     def product(left, right):
         return jnp.dot(left, right, preferred_element_type=jnp.float32)
 
-    for g in range(ngroups):
+    def multiply_cross(j):
+        x = same[firsts[j]]
+        q = firsts[j] ^ mirror
+        at = j * LANES
+        y, yt, z, zt = same[q], plain_turn[q], odd[q], odd_turn[q]
+        put(cross_products, at, x, y, yt)
+        put(cross_products, at + nrow, x, z, zt)
+        put(cross_products, at + 2 * nrow, x, halves_swapped(y), halves_swapped(yt))
+        put(cross_products, at + 3 * nrow, x, halves_swapped(z), halves_swapped(zt))
+
+    def cross_sum(selector, first, last, columns):
+        rows = slice(first * LANES, last * LANES)
+        return product(selector[:, rows], cross_products[rows, columns])
+
+    def self_sum(selector, i, columns):
+        return product(selector[:, i * base : (i + 1) * base], products[i % 2, :, columns])
+
+    real, imag = slice(0, nfreq), slice(nfreq, 2 * nfreq)
+    def collect(i):
+        g = sequence[i]
         here = range(max(g * GROUP, 1), (g + 1) * GROUP)
         span(plain, here[0], len(here), send_a, recv_a.at[g]).wait_recv()
         for k in range(g * GROUP, (g + 1) * GROUP):
             prepare(k)
-        if g < ngroups - 1:
-            multiply_self(products, g)
-            part_re = product(select_re[g], products[:, 0:nfreq])
-            part_im = product(select_im[g], products[:, nfreq : 2 * nfreq])
-            total_re[...] = part_re if g == 0 else total_re[...] + part_re
-            total_im[...] = part_im if g == 0 else total_im[...] + part_im
-        else:
-            multiply_self(last_products, g)
-
-    for j in range(n // 2):
-        x = plain[firsts[j]]
-        q = firsts[j] ^ mirror
-        at = base + j * LANES
-        y, yt, z, zt = plain[q], plain_turn[q], odd[q], odd_turn[q]
-        put(last_products, at, x, y, yt)
-        put(last_products, at + nrow, x, z, zt)
-        put(last_products, at + 2 * nrow, x, halves_swapped(y), halves_swapped(yt))
-        put(last_products, at + 3 * nrow, x, halves_swapped(z), halves_swapped(zt))
-
-    terms_re = total_re[...] + product(last_re[...], last_products[:, 0:nfreq])
-    outgoing[:, :, 0:nfreq] = terms_re.reshape(n, nbins_dev, nfreq).astype(jnp.bfloat16)
-    terms_im = total_im[...] + product(last_im[...], last_products[:, nfreq : 2 * nfreq])
-    outgoing[:, :, nfreq : 2 * nfreq] = terms_im.reshape(n, nbins_dev, nfreq).astype(jnp.bfloat16)
-
-    for k in order:
-        remote(outgoing.at[peer(k)], incoming.at[me], send_b, recv_b, peer(k)).start()
+        multiply_self(products.at[i % 2], g)
+
+    collect(0)
+    collect(1)
+    select_self(0)
+    total_re[...] = self_sum(select_re, 0, real) + self_sum(select_re, 1, real)
+    total_im[...] = self_sum(select_im, 0, imag) + self_sum(select_im, 1, imag)
+    select_self(1)
+    select_cross()
+    collect(2)
+    for j in range(PLANE):
+        multiply_cross(j)
+    total_re[...] += self_sum(select_re, 2, real) + cross_sum(cross_re, 0, PLANE, real)
+    total_im[...] += self_sum(select_im, 2, imag) + cross_sum(cross_im, 0, PLANE, imag)
+    collect(3)
+    for j in range(PLANE, 2 * PLANE):
+        multiply_cross(j)
+    last = ngroups - 1
+    terms_re = (
+        total_re[...]
+        + self_sum(select_re, last, real)
+        + cross_sum(cross_re, PLANE, 2 * PLANE, real)
+    )
+    terms_re = terms_re.reshape(n, nbins_dev, nfreq).astype(jnp.bfloat16)
+    terms_im = (
+        total_im[...]
+        + self_sum(select_im, last, imag)
+        + cross_sum(cross_im, PLANE, 2 * PLANE, imag)
+    )
+    terms_im = terms_im.reshape(n, nbins_dev, nfreq).astype(jnp.bfloat16)
+    outgoing[:, :, real] = terms_re
+    outgoing[:, :, imag] = terms_im
+
+    for i in range(n - 1):
+        target = i + (i + n - me) // n
+        remote(outgoing.at[target], incoming.at[me], send_b, recv_b, target).start()
     incoming[me] = outgoing[me]
     copy_table.wait()
     copy_phase.wait()
@@ -487,7 +525,7 @@
     lags = jnp.sum(lags.reshape(n, nbins_dev, 2 * LAGS) * phases[...], axis=0)
     out_ref[...] = lags[:, :LAGS] + lags[:, LAGS:]
 
-    span(metas, 1, n - 1, send_m, recv_m).wait_send()
+    span(metas, 1, n - 1, send_m, recv_m.at[0]).wait_send()
     span(plain, 1, n - 1, send_a, recv_a.at[0]).wait_send()
     span(incoming, 0, n - 1, send_b, recv_b).wait_send()
 
@@ -499,7 +537,7 @@
     nrow = nchan * nwin * 2
     nbins = n * BINS_DEV
     base = 3 * LANES
-    deep = base + n // 2 * LANES
+    deep = n // 2 * LANES
     scale = 1.0 / (math.sqrt(nfreq_all) * nwin * math.sqrt(PAIRS_DEV // BINS_DEV))
     hbm = pl.BlockSpec(memory_space=pltpu.HBM)
     vmem = pl.BlockSpec(memory_space=pltpu.VMEM)
@@ -524,14 +562,15 @@
             pltpu.VMEM((n, nrow, nfreq), bf16),
             pltpu.VMEM((n, nrow, nfreq), bf16),
             pltpu.VMEM((n, nrow, nfreq), bf16),
+            pltpu.VMEM((n, nrow, nfreq), bf16),
             pltpu.VMEM((2 * nfreq, 2 * LAGS), bf16),
             pltpu.VMEM((n, 1, 2 * LAGS), jnp.float32),
             pltpu.VMEM((n, 8, LANES), jnp.float32),
-            pltpu.VMEM((n // GROUP - 1, nbins, base), bf16),
-            pltpu.VMEM((n // GROUP - 1, nbins, base), bf16),
+            pltpu.VMEM((nbins, n // GROUP * base), bf16),
+            pltpu.VMEM((nbins, n // GROUP * base), bf16),
             pltpu.VMEM((nbins, deep), bf16),
             pltpu.VMEM((nbins, deep), bf16),
-            pltpu.VMEM((base, 2 * nfreq), bf16),
+            pltpu.VMEM((2, base, 2 * nfreq), bf16),
             pltpu.VMEM((deep, 2 * nfreq), bf16),
             pltpu.VMEM((nbins, nfreq), jnp.float32),
             pltpu.VMEM((nbins, nfreq), jnp.float32),
@@ -541,7 +580,7 @@
             dma,
             dma((n // GROUP,)),
             dma,
-            dma,
+            dma((2,)),
             dma,
             dma,
             pltpu.SemaphoreType.REGULAR,
@@ -571,7 +610,8 @@
         P(("grp", "chan")),
     )
     out_specs = P(("grp", "chan"), None)
-    whole_bands = F % (mesh.shape["chan"] * BAND) == 0
+    nblocks = mesh.shape["chan"]
+    whole_bands = F % (nblocks * BAND) == 0 and nblocks == GROUP * PLANE
     return jax.shard_map(
         on_device_slices if whole_bands else on_device_blocks,
         mesh=mesh,

time: 19.8 us -> 19.4 us (0.980)
  Pallas kernels: 18.4 us -> 18 us
    pallas_call x1, Pallas kernels: 18.4 us -> 18 us  [on_device_slices(): pl.pallas_call(functools.partial(kernel, (n, nchan, nwin, nfreq, BINS_DEV...]
where the time goes in v3:
time: 19.4 us; the launch traced here: 19.3 us
  Pallas kernels  18 us (93%)
  between operations  0.66 us (3%)
  local copies, waits for them, and re-layouts  0.62 us (3%)
    pallas_call x1, Pallas kernels, on_device_slices(): pl.pallas_call(functools.partial(kernel, (n, nchan, nwin, nfreq, BINS_DEV...  18 us
    unnamed x1, local copies, waits for them, and re-layouts  0.62 us

profile of v3, /device:TPU:0, one launch (start us, length us, event | category | flops | bytes accessed | tf_op | source)
XLA Modules:
  0.0 19.3 jit_solution(14403580739818213140)
XLA Ops:
  0.7 18.0 %shard_map.82 = f32[8,1024]{1,0:T(8,128)S(1)} custom-call(bf16[4,4,2,4096]{3,2,1,0:T(2,128)(2,1)} %spectra_hbm.1, s32[4,4]{1,0:T(4,128)} %valid_hbm.1, s32[16]{0:T(128)} %partner_hbm.1, s32[32]{0:T(128)} %bin_hbm.1, s32[1]{0:T(128)S(6)} %copy.11.count_hbm, bf16[128,768]{1,0:T(8,128)(2,1)} %constant.6.clone.expand_hbm, ...), custom_call_target="tpu_custom_call" | custom-call | tf_op jit(solution)/shard_map/pallas_call | solution.py:546
  18.7 0.6 %copy.10 = f32[8,1024]{1,0:T(8,128)} copy(f32[8,1024]{1,0:T(8,128)S(1)} %shard_map.82) | data formatting | bytes 65536

commit v4 on v3

--- a/solution.py
+++ b/solution.py
@@ -102,20 +102,26 @@
     return summed * (1.0 / math.sqrt(PAIRS_DEV // BINS_DEV))
 
 
+def lag_span():
+    return LAGS // 2 + LANES
+
+
+def interleaved(cos, sin):
+    tiled = [part.reshape(part.shape[0], -1, 1, LANES) for part in (cos, sin)]
+    return np.concatenate(tiled, axis=2).reshape(cos.shape[0], -1)
+
+
 def base_table(nfreq):
-    shifts = np.arange(LAGS) - LAGS // 2
+    shifts = np.arange(lag_span())
     angle = np.mod(np.arange(nfreq)[:, None] * shifts[None, :], 2 * F) * (2.0 * math.pi / (2 * F))
-    cos, sin = np.cos(angle), np.sin(angle)
-    return np.concatenate(
-        [np.concatenate([cos, sin], axis=1), np.concatenate([-sin, cos], axis=1)], axis=0
-    ).astype(ml_dtypes.bfloat16)
+    return interleaved(np.cos(angle), np.sin(angle)).astype(ml_dtypes.bfloat16)
 
 
 def slice_phases(nslices, nfreq, scale):
-    shifts = np.arange(LAGS) - LAGS // 2
+    shifts = np.arange(lag_span())
     first = np.arange(nslices) * nfreq
     angle = np.mod(first[:, None] * shifts[None, :], 2 * F) * (2.0 * math.pi / (2 * F))
-    both = np.concatenate([np.cos(angle), -np.sin(angle)], axis=1) * scale
+    both = interleaved(np.cos(angle), np.sin(angle)) * scale
     return both.astype(np.float32)[:, None, :]
 
 
@@ -520,10 +526,25 @@
     copy_phase.wait()
     span(incoming, 0, n - 1, send_b, recv_b).wait_recv()
 
-    stacked = incoming[...].astype(jnp.float32).reshape(nbins, 2 * nfreq).astype(jnp.bfloat16)
-    lags = product(stacked, table[...])
-    lags = jnp.sum(lags.reshape(n, nbins_dev, 2 * LAGS) * phases[...], axis=0)
-    out_ref[...] = lags[:, :LAGS] + lags[:, LAGS:]
+    arrived = incoming[...].astype(jnp.float32).reshape(nbins, 2 * nfreq).astype(jnp.bfloat16)
+    stacked = jnp.concatenate([arrived[:, real], arrived[:, imag]], axis=0)
+    zero_lag = LAGS // 2
+    lane = lax.broadcasted_iota(jnp.int32, (nbins_dev, LANES), 1)
+    backward = (LANES - lane) % LANES
+    mirrored = []
+    for a in range(lag_span() // LANES):
+        both = slice(2 * a * LANES, 2 * (a + 1) * LANES)
+        lags = product(stacked, table[:, both]).reshape(2, n, nbins_dev, 2 * LANES)
+        cos, sin = phases[:, :, both][:, :, :LANES], phases[:, :, both][:, :, LANES:]
+        even_part = jnp.sum(lags[0, :, :, :LANES] * cos - lags[0, :, :, LANES:] * sin, axis=0)
+        odd_part = jnp.sum(lags[1, :, :, LANES:] * cos + lags[1, :, :, :LANES] * sin, axis=0)
+        if a < zero_lag // LANES:
+            out_ref[:, zero_lag + a * LANES : zero_lag + (a + 1) * LANES] = even_part - odd_part
+        mirrored.append(even_part + odd_part)
+    for a in range(zero_lag // LANES):
+        high = mirrored[zero_lag // LANES - a]
+        low = jnp.take_along_axis(mirrored[zero_lag // LANES - a - 1], backward, axis=1)
+        out_ref[:, a * LANES : (a + 1) * LANES] = jnp.where(lane == 0, high, low)
 
     span(metas, 1, n - 1, send_m, recv_m.at[0]).wait_send()
     span(plain, 1, n - 1, send_a, recv_a.at[0]).wait_send()
@@ -563,8 +584,8 @@
             pltpu.VMEM((n, nrow, nfreq), bf16),
             pltpu.VMEM((n, nrow, nfreq), bf16),
             pltpu.VMEM((n, nrow, nfreq), bf16),
-            pltpu.VMEM((2 * nfreq, 2 * LAGS), bf16),
-            pltpu.VMEM((n, 1, 2 * LAGS), jnp.float32),
+            pltpu.VMEM((nfreq, 2 * lag_span()), bf16),
+            pltpu.VMEM((n, 1, 2 * lag_span()), jnp.float32),
             pltpu.VMEM((n, 8, LANES), jnp.float32),
             pltpu.VMEM((nbins, n // GROUP * base), bf16),
             pltpu.VMEM((nbins, n // GROUP * base), bf16),

time: 19.4 us -> 19.4 us (level)
  no operation moved by 1% of the time
where the time goes in v4:
time: 19.4 us; the launch traced here: 19.2 us
  Pallas kernels  17.9 us (92%)
  between operations  0.66 us (3%)
  local copies, waits for them, and re-layouts  0.62 us (3%)
    pallas_call x1, Pallas kernels, on_device_slices(): pl.pallas_call(functools.partial(kernel, (n, nchan, nwin, nfreq, BINS_DEV...  17.9 us
    unnamed x1, local copies, waits for them, and re-layouts  0.62 us

profile of v4, /device:TPU:0, one launch (start us, length us, event | category | flops | bytes accessed | tf_op | source)
XLA Modules:
  0.0 19.2 jit_solution(5536517522882620739)
XLA Ops:
  0.7 17.9 %shard_map.82 = f32[8,1024]{1,0:T(8,128)S(1)} custom-call(bf16[4,4,2,4096]{3,2,1,0:T(2,128)(2,1)} %spectra_hbm.1, s32[4,4]{1,0:T(4,128)} %valid_hbm.1, s32[16]{0:T(128)} %partner_hbm.1, s32[32]{0:T(128)} %bin_hbm.1, s32[1]{0:T(128)S(6)} %copy.11.count_hbm, bf16[128,768]{1,0:T(8,128)(2,1)} %constant.6.clone.expand_hbm, ...), custom_call_target="tpu_custom_call" | custom-call | tf_op jit(solution)/shard_map/pallas_call | solution.py:567
  18.6 0.6 %copy.10 = f32[8,1024]{1,0:T(8,128)} copy(f32[8,1024]{1,0:T(8,128)S(1)} %shard_map.82) | data formatting | bytes 65536

commit v5 on v4

--- a/solution.py
+++ b/solution.py
@@ -254,9 +254,6 @@
             )
         )
     ]
-    copy_own.start()
-    for copy in small[:3]:
-        copy.start()
     plane = me // PLANE
     is_last = plane == n // PLANE - 1
     barrier = pltpu.get_barrier_semaphore()
@@ -274,7 +271,8 @@
     def _():
         signal(barrier, range(n - 1, 0, -1))
 
-    for copy in small[3:]:
+    copy_own.start()
+    for copy in small:
         copy.start()
     copy_table.start()
     copy_phase.start()

time: 19.4 us -> 19.4 us (level)
  no operation moved by 1% of the time
where the time goes in v5:
time: 19.4 us; the launch traced here: 19.2 us
  Pallas kernels  17.9 us (92%)
  between operations  0.66 us (3%)
  local copies, waits for them, and re-layouts  0.62 us (3%)
    pallas_call x1, Pallas kernels, on_device_slices(): pl.pallas_call(functools.partial(kernel, (n, nchan, nwin, nfreq, BINS_DEV...  17.9 us
    unnamed x1, local copies, waits for them, and re-layouts  0.62 us

profile of v5, /device:TPU:0, one launch (start us, length us, event | category | flops | bytes accessed | tf_op | source)
XLA Modules:
  0.0 19.2 jit_solution(9926023762301195026)
XLA Ops:
  0.7 17.9 %shard_map.82 = f32[8,1024]{1,0:T(8,128)S(1)} custom-call(bf16[4,4,2,4096]{3,2,1,0:T(2,128)(2,1)} %spectra_hbm.1, s32[4,4]{1,0:T(4,128)} %valid_hbm.1, s32[16]{0:T(128)} %partner_hbm.1, s32[32]{0:T(128)} %bin_hbm.1, s32[1]{0:T(128)S(6)} %copy.11.count_hbm, bf16[128,768]{1,0:T(8,128)(2,1)} %constant.6.clone.expand_hbm, ...), custom_call_target="tpu_custom_call" | custom-call | tf_op jit(solution)/shard_map/pallas_call | solution.py:565
  18.6 0.6 %copy.10 = f32[8,1024]{1,0:T(8,128)} copy(f32[8,1024]{1,0:T(8,128)S(1)} %shard_map.82) | data formatting | bytes 65536

commit v6 on v5

--- a/solution.py
+++ b/solution.py
@@ -276,6 +276,16 @@
         copy.start()
     copy_table.start()
     copy_phase.start()
+    near = [7, 6, 5, 4]
+    middle = [11, 10, 9, 8]
+    far = [15, 14, 13, 12]
+    inside = [3, 2, 1]
+
+    @pl.when(is_last)
+    def _():
+        pl.semaphore_wait(barrier, 3 * PLANE)
+        signal(ready, far + middle + near)
+
     for copy in small[:3]:
         copy.wait()
 
@@ -318,10 +328,6 @@
         for k in ks:
             act(k)
 
-    near = [7, 6, 5, 4]
-    middle = [11, 10, 9, 8]
-    far = [15, 14, 13, 12]
-    inside = [3, 2, 1]
     copy_own.wait()
 
     @pl.when(jnp.logical_not(is_last))
@@ -336,8 +342,6 @@
 
     @pl.when(is_last)
     def _():
-        pl.semaphore_wait(barrier, 3 * PLANE)
-        signal(ready, far + middle + near)
         each(send_meta, far + middle + near)
         for k in far + middle + near:
             whiten_slice(peer(k))

time: 19.4 us -> 19.4 us (level)
  no operation moved by 1% of the time
where the time goes in v6:
time: 19.4 us; the launch traced here: 19.2 us
  Pallas kernels  17.9 us (92%)
  between operations  0.66 us (3%)
  local copies, waits for them, and re-layouts  0.62 us (3%)
    pallas_call x1, Pallas kernels, on_device_slices(): pl.pallas_call(functools.partial(kernel, (n, nchan, nwin, nfreq, BINS_DEV...  17.9 us
    unnamed x1, local copies, waits for them, and re-layouts  0.62 us

profile of v6, /device:TPU:0, one launch (start us, length us, event | category | flops | bytes accessed | tf_op | source)
XLA Modules:
  0.0 19.2 jit_solution(4547635813493419355)
XLA Ops:
  0.7 17.9 %shard_map.82 = f32[8,1024]{1,0:T(8,128)S(1)} custom-call(bf16[4,4,2,4096]{3,2,1,0:T(2,128)(2,1)} %spectra_hbm.1, s32[4,4]{1,0:T(4,128)} %valid_hbm.1, s32[16]{0:T(128)} %partner_hbm.1, s32[32]{0:T(128)} %bin_hbm.1, s32[1]{0:T(128)S(6)} %copy.11.count_hbm, bf16[128,768]{1,0:T(8,128)(2,1)} %constant.6.clone.expand_hbm, ...), custom_call_target="tpu_custom_call" | custom-call | tf_op jit(solution)/shard_map/pallas_call | solution.py:569
  18.6 0.6 %copy.10 = f32[8,1024]{1,0:T(8,128)} copy(f32[8,1024]{1,0:T(8,128)S(1)} %shard_map.82) | data formatting | bytes 65536

commit v7 on v5

--- a/solution.py
+++ b/solution.py
@@ -351,7 +351,7 @@
     @pl.when(plane == 2)
     def _():
         each(send_meta, far + middle + inside)
-        each(send_white, far + middle)
+        each(send_white, middle + far)
         pl.semaphore_wait(ready, PLANE)
         signal(token, near[-1:])
         each(send_meta, near)

time: 19.4 us -> 19.4 us (level)
  no operation moved by 1% of the time
where the time goes in v7:
time: 19.4 us; the launch traced here: 19.2 us
  Pallas kernels  17.9 us (92%)
  between operations  0.66 us (3%)
  local copies, waits for them, and re-layouts  0.62 us (3%)
    pallas_call x1, Pallas kernels, on_device_slices(): pl.pallas_call(functools.partial(kernel, (n, nchan, nwin, nfreq, BINS_DEV...  17.9 us
    unnamed x1, local copies, waits for them, and re-layouts  0.62 us

profile of v7, /device:TPU:0, one launch (start us, length us, event | category | flops | bytes accessed | tf_op | source)
XLA Modules:
  0.0 19.2 jit_solution(9349254459963352610)
XLA Ops:
  0.7 17.9 %shard_map.82 = f32[8,1024]{1,0:T(8,128)S(1)} custom-call(bf16[4,4,2,4096]{3,2,1,0:T(2,128)(2,1)} %spectra_hbm.1, s32[4,4]{1,0:T(4,128)} %valid_hbm.1, s32[16]{0:T(128)} %partner_hbm.1, s32[32]{0:T(128)} %bin_hbm.1, s32[1]{0:T(128)S(6)} %copy.11.count_hbm, bf16[128,768]{1,0:T(8,128)(2,1)} %constant.6.clone.expand_hbm, ...), custom_call_target="tpu_custom_call" | custom-call | tf_op jit(solution)/shard_map/pallas_call | solution.py:565
  18.6 0.6 %copy.10 = f32[8,1024]{1,0:T(8,128)} copy(f32[8,1024]{1,0:T(8,128)S(1)} %shard_map.82) | data formatting | bytes 65536
